TPU v7x, 32 devices: a whole 2x2x4 slice. The times are simulated.
32 devices in a mesh: seq: 8 (over z, x), head: 4 (over y, core).
Axes of the slice: x: 2, y: 2, z: 4, core: 2. Of those that a mesh axis runs over, the one named last changes fastest.
Arguments:
- queries: bfloat16 [1024, 4096], P('seq', 'head'), may hold values from -6 to 6
- keys: bfloat16 [1024, 4096], P('seq', 'head'), may hold values from -6 to 6
- values: bfloat16 [1024, 4096], P('seq', 'head'), may hold values from -3 to 3
- decay_codes: int32 [1024, 32], P('seq', 'head'), may hold values from 0 to 2048
- out_weight: bfloat16 [4096, 3072], P('head'), may hold values from -0.09375 to 0.09375
- out_grad: bfloat16 [1024, 3072], P('seq', 'head'), may hold values from -6 to 6
Outputs:
- mixed: bfloat16 [1024, 3072], P('seq', 'head')
- query_gradient: bfloat16 [1024, 4096], P('seq', 'head')
- key_grad: bfloat16 [1024, 4096], P('seq', 'head')
- value_gradient: bfloat16 [1024, 4096], P('seq', 'head')
All inputs are finite; a program needn't handle non-finite values.
Results may differ from a plain program's by a relative error of at most 0.014.
Values may be sent and summed in bfloat16 or wider, within the bound.
No kernel may reach another device: no remote copies, remote signals or barrier semaphores. Data moves between devices by JAX's collectives and lax.ppermute only.
A program may use at most 128 MiB of HBM per device.

v0:
```python
import jax
import jax.numpy as jnp
from jax import lax
from jax.sharding import PartitionSpec as P


def prefix(value, axis, join, neutral):
    count, mine = (lax.axis_size(axis), lax.axis_index(axis))
    pieces = jax.tree.map(lambda part: lax.all_gather(part, axis), value)
    subtotal = jax.tree.map(
        lambda part, zero: jnp.full_like(part, 0) + jnp.asarray(zero, part.dtype), value, neutral
    )

    def prefix_step(position, subtotal):
        longer = join(subtotal, jax.tree.map(lambda part: part[position], pieces))
        return jax.tree.map(lambda new, old: jnp.where(position < mine, new, old), longer, subtotal)

    return lax.fori_loop(0, count - 1, prefix_step, subtotal)


def entering(array, axis, combine, identity):
    devices, place = (lax.axis_size(axis), lax.axis_index(axis))
    everything = jax.tree.map(
        lambda part, kind: lax.all_gather(part.astype(kind), axis),
        array,
        (jnp.bfloat16, jnp.bfloat16),
    )
    start = jax.tree.map(
        lambda part, zero: jnp.broadcast_to(jnp.asarray(zero, part.dtype), part.shape),
        array,
        identity,
    )

    def entering_step(k, before):
        at = devices - 1 - k
        reached = at > place
        new = combine(
            before, jax.tree.map(lambda part, own: part[at].astype(own.dtype), everything, array)
        )
        return jax.tree.map(lambda a, b: jnp.where(reached, a, b), new, before)

    return lax.fori_loop(0, devices, entering_step, start)


def block_mask(cum_log):
    block_len = cum_log.shape[0]
    log_gap = cum_log.T[:, :, None] - cum_log.T[:, None, :]
    lower_part = (jnp.arange(block_len)[:, None] >= jnp.arange(block_len)[None, :])[None]
    return jnp.where(lower_part, jnp.exp(jnp.where(lower_part, log_gap, 0.0)), 0.0)


def combine(earlier, later):
    return (earlier[0] * later[0], later[0][:, None, None] * earlier[1] + later[1])


def local(queries, keys, values, decay_codes, out_weight, out_grad):
    tok_rows = queries.shape[0]
    head_count = decay_codes.shape[1]
    head_width = queries.shape[1] // head_count
    att_scale = 1.0 / head_width
    grad_flat = lax.dot_general(
        lax.all_gather(out_grad, "head", axis=1, tiled=True),
        out_weight,
        (((1,), (1,)), ((), ())),
        preferred_element_type=jnp.float32,
    ).astype(jnp.bfloat16)

    def to_heads(array):
        return array.reshape(tok_rows, head_count, head_width)

    query_h = to_heads(queries)
    key_h = to_heads(keys)
    value_h = to_heads(values)
    grad_h = to_heads(grad_flat)
    cum_log = jnp.cumsum(jnp.log(1.0 - decay_codes.astype(jnp.float32) / 4096.0), axis=0)
    decay_mask = block_mask(cum_log)
    rise_decay = jnp.exp(cum_log)[:, :, None]
    fall_decay = jnp.exp(cum_log[-1][None, :] - cum_log)[:, :, None]
    total_decay = jnp.exp(cum_log[-1])
    k_fall = (fall_decay * key_h.astype(jnp.float32)).astype(jnp.bfloat16)
    summary_fwd = jnp.einsum("thd,the->hde", k_fall, value_h, preferred_element_type=jnp.float32)
    q_rise = (att_scale * rise_decay * query_h.astype(jnp.float32)).astype(jnp.bfloat16)
    summary_bwd = jnp.einsum("shd,she->hde", q_rise, grad_h, preferred_element_type=jnp.float32)
    identity = (
        jnp.ones((head_count,), jnp.float32),
        jnp.zeros((head_count, head_width, head_width), jnp.float32),
    )
    passed_fwd, state_in = prefix((total_decay, summary_fwd), "seq", combine, identity)
    passed_bwd, carry_in = entering((total_decay, summary_bwd), "seq", combine, identity)
    scores = jnp.einsum("she,the->hst", query_h, key_h, preferred_element_type=jnp.float32)
    attn = (att_scale * scores * decay_mask).astype(jnp.bfloat16)
    pscores = jnp.einsum("she,the->hst", grad_h, value_h, preferred_element_type=jnp.float32)
    pmat = (att_scale * pscores * decay_mask).astype(jnp.bfloat16)
    g_rise = (att_scale * rise_decay * grad_h.astype(jnp.float32)).astype(jnp.bfloat16)
    v_fall = (fall_decay * value_h.astype(jnp.float32)).astype(jnp.bfloat16)
    local_out = jnp.einsum("hst,the->she", attn, value_h, preferred_element_type=jnp.float32)
    local_qgrad = jnp.einsum("hst,thd->shd", pmat, key_h, preferred_element_type=jnp.float32)
    local_kgrad = jnp.einsum("hst,shd->thd", pmat, query_h, preferred_element_type=jnp.float32)
    local_vgrad = jnp.einsum("hst,she->the", attn, grad_h, preferred_element_type=jnp.float32)
    state_b = state_in.astype(jnp.bfloat16)
    carry_b = carry_in.astype(jnp.bfloat16)
    attn_out = local_out + jnp.einsum(
        "shd,hde->she", q_rise, state_b, preferred_element_type=jnp.float32
    )
    query_gradient = local_qgrad + jnp.einsum(
        "she,hde->shd", g_rise, state_b, preferred_element_type=jnp.float32
    )
    key_grad = local_kgrad + jnp.einsum(
        "the,hde->thd", v_fall, carry_b, preferred_element_type=jnp.float32
    )
    value_gradient = local_vgrad + jnp.einsum(
        "thd,hde->the", k_fall, carry_b, preferred_element_type=jnp.float32
    )
    attn_flat = attn_out.astype(jnp.bfloat16).reshape(tok_rows, -1)
    partial_out = jnp.dot(attn_flat, out_weight, preferred_element_type=jnp.float32)
    mixed = lax.psum_scatter(
        partial_out.astype(jnp.bfloat16), "head", scatter_dimension=1, tiled=True
    )
    flat_width = queries.shape[1]
    return (
        mixed,
        query_gradient.astype(jnp.bfloat16).reshape(tok_rows, flat_width),
        key_grad.astype(jnp.bfloat16).reshape(tok_rows, flat_width),
        value_gradient.astype(jnp.bfloat16).reshape(tok_rows, flat_width),
    )


def solution(mesh):
    placed = (
        P("seq", "head"),
        P("seq", "head"),
        P("seq", "head"),
        P("seq", "head"),
        P("head", None),
        P("seq", "head"),
    )
    return jax.shard_map(
        local,
        mesh=mesh,
        in_specs=placed,
        out_specs=(P("seq", "head"), P("seq", "head"), P("seq", "head"), P("seq", "head")),
        check_vma=False,
    )
```

profile of v0, /device:TPU:0, one launch (start us, length us, event | category | flops | bytes accessed | tf_op | source)
XLA Modules:
  0.0 168.2 jit_solution(11531859500850806780)
XLA Ops:
  8.3 2.2 %fusion.16 = f32[8,128,128]{2,1,0:T(8,128)} fusion(f32[128,8]{0,1:T(8,128)S(1)} %copy.70, bf16[128,1024]{1,0:T(8,128)(2,1)S(1)} %copy-done, bf16[128,1024]{1,0:T(8,128)(2,1)} %param.11), kind=kOutput, calls=%fused_computation.37 | convolution fusion | flops 33947648 | bytes 1052672 | tf_op jit(solution)/shard_map/thd,the->hde/dot_general | solution.py:81
  10.7 1.1 copy.97
  11.8 10.3 %all_gather.26 = bf16[128,3072]{1,0:T(8,128)(2,1)S(1)} all-gather(bf16[128,768]{1,0:T(8,128)(2,1)} %param.15), channel_id=1, replica_groups=mesh['seq'=8,'head'=4] {'head'}, dimensions={1}, use_global_device_ids=true | all-gather | bytes 983040 | tf_op jit(solution)/shard_map/all_gather | solution.py:62
  22.1 5.1 %convolution_convert_fusion.2 = bf16[128,1024]{1,0:T(8,128)(2,1)S(1)} fusion(bf16[128,3072]{1,0:T(8,128)(2,1)S(1)} %all_gather.26, bf16[1024,3072]{1,0:T(8,128)(2,1)} %param.14), kind=kOutput, calls=%fused_computation.24 | convolution fusion | flops 805437440 | bytes 7340032 | tf_op jit(solution)/shard_map/dot_general | solution.py:61
  27.4 1.0 convolution_convert_fusion.1
  28.6 1.1 fusion.7
  30.0 21.2 %all-gather.2 = f32[8,1,8]{2,1,0:T(1,128)S(1)} all-gather(f32[1,1,8]{2,1,0:T(1,128)S(1)} %get-tuple-element.302), channel_id=1, replica_groups=mesh['seq'=8,'head'=4] {'seq'}, dimensions={0}, use_global_device_ids=true | all-gather | bytes 288 | tf_op jit(solution)/shard_map/all_gather | solution.py:9
  51.4 17.2 %all-gather.3 = bf16[8,1,8]{2,1,0:T(2,128)(2,1)S(1)} all-gather(bf16[1,1,8]{2,1,0:T(2,128)(2,1)S(1)} %get-tuple-element.300), channel_id=1, replica_groups=mesh['seq'=8,'head'=4] {'seq'}, dimensions={0}, use_global_device_ids=true | all-gather | bytes 144 | tf_op jit(solution)/shard_map/all_gather | solution.py:24
  68.5 1.2 fusion.35
  69.7 16.6 %all-gather.7.cloned.1.call-done = f32[64,128,128]{2,1,0:T(8,128)} async-done(((f32[8,128,128]{2,1,0:T(8,128)}), f32[64,128,128]{2,1,0:T(8,128)}) %all-gather.7.cloned.1.call-update) | async-done | bytes 4194320 | tf_op jit(solution)/shard_map/all_gather | solution.py:9
  86.3 8.5 %while.30 = (s32[]{:T(128)}, f32[8,128,128]{2,1,0:T(8,128)S(1)}, s32[]{:T(128)}, f32[8,8]{1,0:T(8,128)S(1)}, f32[8,8,128,128]{3,2,1,0:T(8,128)}, /*index=5*/s32[]{:T(128)}, s32[]{:T(128)}) while((s32[]{:T(128)}, f32[8,128,128]{2,1,0:T(8,128)S(1)}, s32[]{:T(128)}, f32[8,8]{1,0:T(8,128)S(1)}, f32[8,8,128,128]{3,2,1,0:T(8,128)}, ...), condition=%wide.region_2.3_spmd.clone, body=%wide.region_1.2_spmd.clone.sunk | while | flops 524292 | bytes 1573073 | solution.py:18
  86.4 1.2 fusion.59
  87.6 1.2 fusion.59
  88.8 1.2 fusion.59
  90.0 1.2 fusion.59
  91.2 1.2 fusion.59
  92.4 1.2 fusion.59
  93.6 1.2 fusion.59
  95.1 1.3 fusion.12
  96.4 4.7 %convolution_convert_fusion = bf16[128,3072]{1,0:T(8,128)(2,1)} fusion(bf16[128,1024]{0,1:T(8,128)(2,1)S(1)} %bitcast.131, bf16[1024,3072]{1,0:T(8,128)(2,1)} %param.14), kind=kOutput, calls=%fused_computation.6 | convolution fusion | flops 805699584 | bytes 7340032 | tf_op jit(solution)/shard_map/dot_general | solution.py:115
  101.2 35.6 %all-gather.9.cloned.1.call-done = bf16[64,128,128]{2,1,0:T(8,128)(2,1)} async-done(((bf16[8,128,128]{2,1,0:T(8,128)(2,1)}), bf16[64,128,128]{2,1,0:T(8,128)(2,1)}) %all-gather.9.cloned.1.call-update) | async-done | bytes 2097168 | tf_op jit(solution)/shard_map/all_gather | solution.py:24
  136.7 9.1 %while.31 = (s32[]{:T(128)}, f32[8,128,128]{2,1,0:T(8,128)S(1)}, s32[]{:T(128)}, bf16[8,8]{1,0:T(8,128)(2,1)S(1)}, bf16[8,8,128,128]{3,2,1,0:T(8,128)(2,1)}, /*index=5*/s32[]{:T(128)}, s32[]{:T(128)}, s32[]{:T(128)}, s32[]{:T(128)}) while((s32[]{:T(128)}, f32[8,128,128]{2,1,0:T(8,128)S(1)}, s32[]{:T(128)}, ...), condition=%wide.region_5.6_spmd.clone, body=%wide.region_4.5_spmd.clone.sunk | while | flops 655376 | bytes 1310975 | solution.py:42
  136.7 1.1 fusion.60
  137.9 1.1 fusion.60
  139.0 1.1 fusion.60
  140.1 1.1 fusion.60
  141.3 1.1 fusion.60
  142.4 1.1 fusion.60
  143.6 1.1 fusion.60
  144.7 1.1 fusion.60
  146.2 0.9 copy.89
  149.8 11.9 %reduce-scatter.2.cloned.1.call-done = bf16[128,768]{1,0:T(8,128)(2,1)} async-done(((bf16[128,3072]{1,0:T(8,128)(2,1)}), bf16[128,768]{1,0:T(8,128)(2,1)}) %reduce-scatter.2.cloned.1.call-update) | async-done | bytes 196624 | tf_op jit(solution)/shard_map/reduce_scatter | solution.py:116
  (47 shorter events, 5.5 us)
Async XLA Ops:
  7.2 1.2 copy-start
  7.2 79.2 %all-gather.7.cloned.1.call-start = ((), (), s32[]{:S(2)}) async-start(), calls=%async_computation.2 | async-start | bytes 4718592 | tf_op jit(solution)/shard_map/all_gather | solution.py:9
  8.1 20.5 %copy-start.1 = (bf16[128,1024]{1,0:T(8,128)(2,1)S(1)}, bf16[128,1024]{1,0:T(8,128)(2,1)}, u32[]{:S(2)}) copy-start(bf16[128,1024]{1,0:T(8,128)(2,1)} %param.11) | copy-start | bytes 786436
  10.6 126.1 %all-gather.9.cloned.1.call-start = ((), (), s32[]{:S(2)}) async-start(), calls=%async_computation.3 | async-start | bytes 2359296 | tf_op jit(solution)/shard_map/all_gather | solution.py:24
  28.4 133.2 %reduce-scatter.2.cloned.1.call-start = ((), (), s32[]{:S(2)}) async-start(), calls=%async_computation.1 | async-start | bytes 983040 | tf_op jit(solution)/shard_map/reduce_scatter | solution.py:116
Sparse Core Ops, SparseCore 0:
  10.7 75.5 all-gather.6
  89.0 47.6 all-gather.8
  139.8 21.7 reduce-scatter.1
where the time goes:
time: 169 us; the launch traced here: 168 us
  waiting for transfers between devices  64.1 us (38%)
  blocking collectives  48.7 us (29%)
  matrix products  18.7 us (11%)
  other arithmetic  18 us (11%)
  between operations  13.9 us (8%)
  local copies, waits for them, and re-layouts  4.15 us (2%)
    all_gather x1, waiting for transfers between devices, entering(): lax.all_gather(part.astype(kind), axis)  35.6 us
    all_gather x1, blocking collectives, prefix(): pieces = jax.tree.map(lambda part: lax.all_gather(part, axis), value)  21.2 us
    all_gather x1, blocking collectives, entering(): lax.all_gather(part.astype(kind), axis)  17.2 us
    all_gather x1, waiting for transfers between devices, prefix(): pieces = jax.tree.map(lambda part: lax.all_gather(part, axis), value)  16.6 us
    reduce_scatter x1, waiting for transfers between devices, local(): lax.psum_scatter(partial_out.astype(jnp.bfloat16), 'head', scatter_dimens...  11.9 us
    all_gather x1, blocking collectives, local(): lax.all_gather(out_grad, 'head', axis=1, tiled=True)  10.3 us
    select_n x8, other arithmetic, entering_step(): return jax.tree.map(lambda a, b: jnp.where(reached, a, b), new, before)  8.77 us
    select_n x7, other arithmetic, prefix_step(): jnp.where(position < mine, new, old)  8.22 us
  transfers between devices with their start and end apart: 3, of which 3 were waited for; matrix products, arithmetic and copies ran while one was open for 22% of the time, Pallas kernels for 0%

commit v1 on v0

--- a/solution.py
+++ b/solution.py
@@ -1,7 +1,20 @@
+import functools
 import jax
 import jax.numpy as jnp
 from jax import lax
 from jax.sharding import PartitionSpec as P
+
+
+def cut_the_panel(slab_in, k_dim):
+    local_now = jax.lax.axis_size("head")
+    b_next = jnp.concatenate([slab_in] * local_now, axis=k_dim)
+    k_now = jax.lax.all_to_all(
+        b_next, axis_name="head", split_axis=k_dim, concat_axis=k_dim, tiled=True
+    )
+    return k_now
+
+
+store_tails = functools.partial(cut_the_panel, k_dim=1)
 
 
 def prefix(value, axis, join, neutral):
@@ -59,7 +72,7 @@
     head_width = queries.shape[1] // head_count
     att_scale = 1.0 / head_width
     grad_flat = lax.dot_general(
-        lax.all_gather(out_grad, "head", axis=1, tiled=True),
+        store_tails(out_grad),
         out_weight,
         (((1,), (1,)), ((), ())),
         preferred_element_type=jnp.float32,

time: 169 us -> 169 us (level)
  blocking collectives: 48.7 us -> 38.4 us
  waiting for transfers between devices: 64.1 us -> 71 us
  starting transfers between devices: 0.12 us -> 4.35 us
  matrix products: 18.7 us -> 16.8 us
    all_gather x1 -> x0, blocking collectives: 10.3 us -> none  [local(): lax.all_gather(out_grad, 'head', axis=1, tiled=True)]
    all_gather x1, waiting for transfers between devices: 16.6 us -> 22.7 us  [prefix(): pieces = jax.tree.map(lambda part: lax.all_gather(part, axis), value)]
    all_gather x1, blocking collectives: 17.2 us -> 21.9 us  [entering(): lax.all_gather(part.astype(kind), axis)]
    all_gather x1, blocking collectives: 21.2 us -> 16.5 us  [prefix(): pieces = jax.tree.map(lambda part: lax.all_gather(part, axis), value)]
    all_to_all x0 -> x1, starting transfers between devices: none -> 4.26 us  [cut_the_panel(): jax.lax.all_to_all(b_next, axis_name='head', split_axis=k_dim, concat_axi...]
  transfers between devices with their start and end apart: 3 -> 4, of which waited for: 3 -> 3; matrix products, arithmetic and copies ran while one was open for 22% -> 22% of each run, Pallas kernels for 0% -> 0%
where the time goes in v1:
time: 169 us; the launch traced here: 168 us
  waiting for transfers between devices  71 us (42%)
  blocking collectives  38.4 us (23%)
  other arithmetic  18.1 us (11%)
  matrix products  16.8 us (10%)
  between operations  13.9 us (8%)
  local copies, waits for them, and re-layouts  4.96 us (3%)
  starting transfers between devices  4.35 us (3%)
    all_gather x1, waiting for transfers between devices, entering(): lax.all_gather(part.astype(kind), axis)  36.4 us
    all_gather x1, waiting for transfers between devices, prefix(): pieces = jax.tree.map(lambda part: lax.all_gather(part, axis), value)  22.7 us
    all_gather x1, blocking collectives, entering(): lax.all_gather(part.astype(kind), axis)  21.9 us
    all_gather x1, blocking collectives, prefix(): pieces = jax.tree.map(lambda part: lax.all_gather(part, axis), value)  16.5 us
    reduce_scatter x1, waiting for transfers between devices, local(): lax.psum_scatter(partial_out.astype(jnp.bfloat16), 'head', scatter_dimens...  11.8 us
    select_n x8, other arithmetic, entering_step(): return jax.tree.map(lambda a, b: jnp.where(reached, a, b), new, before)  8.77 us
    select_n x7, other arithmetic, prefix_step(): jnp.where(position < mine, new, old)  8.22 us
    dot_general x1, matrix products, local(): lax.dot_general(store_tails(out_grad), out_weight, (((1,), (1,)), ((), ()...  5.03 us
  transfers between devices with their start and end apart: 4, of which 3 were waited for; matrix products, arithmetic and copies ran while one was open for 22% of the time, Pallas kernels for 0%

profile of v1, /device:TPU:0, one launch (start us, length us, event | category | flops | bytes accessed | tf_op | source)
XLA Modules:
  0.0 168.1 jit_solution(6873466792300278797)
XLA Ops:
  8.3 2.2 %fusion.16 = f32[8,128,128]{2,1,0:T(8,128)} fusion(f32[128,8]{0,1:T(8,128)S(1)} %copy.97, bf16[128,1024]{1,0:T(8,128)(2,1)S(1)} %copy-done, bf16[128,1024]{1,0:T(8,128)(2,1)} %param.11), kind=kOutput, calls=%fused_computation.38 | convolution fusion | flops 33947648 | bytes 1052672 | tf_op jit(solution)/shard_map/thd,the->hde/dot_general | solution.py:94
  10.9 1.2 copy.109
  12.0 4.3 %all-to-all-start = ((bf16[128,4,768]{2,0,1:T(8,128)(2,1)}), bf16[128,4,768]{2,0,1:T(8,128)(2,1)S(1)}, u32[]{:S(2)}, u32[]{:S(2)}) async-start(bf16[128,4,768]{2,0,1:T(8,128)(2,1)} %copy.109), calls=%async_computation.1 | async-start | bytes 1572864 | tf_op jit(solution)/shard_map/all_to_all | solution.py:11
  16.6 21.9 %all-gather.3 = bf16[8,1,8]{2,1,0:T(2,128)(2,1)S(1)} all-gather(bf16[1,1,8]{2,1,0:T(2,128)(2,1)S(1)} %get-tuple-element.304), channel_id=1, replica_groups=mesh['seq'=8,'head'=4] {'seq'}, dimensions={0}, use_global_device_ids=true | all-gather | bytes 144 | tf_op jit(solution)/shard_map/all_gather | solution.py:37
  38.5 16.5 %all-gather.2 = f32[8,1,8]{2,1,0:T(1,128)S(1)} all-gather(f32[1,1,8]{2,1,0:T(1,128)S(1)} %get-tuple-element.306), channel_id=1, replica_groups=mesh['seq'=8,'head'=4] {'seq'}, dimensions={0}, use_global_device_ids=true | all-gather | bytes 288 | tf_op jit(solution)/shard_map/all_gather | solution.py:22
  55.1 1.0 fusion.7
  56.5 5.0 %convolution_convert_fusion.2 = bf16[128,1024]{1,0:T(8,128)(2,1)S(1)} fusion(bf16[128,3072]{0,1:T(8,128)(2,1)S(1)} %bitcast.133, bf16[1024,3072]{1,0:T(8,128)(2,1)} %param.14), kind=kOutput, calls=%fused_computation.24 | convolution fusion | flops 805437440 | bytes 7340032 | tf_op jit(solution)/shard_map/dot_general | solution.py:74
  61.7 1.0 convolution_convert_fusion.1
  63.6 22.7 %all-gather.7.cloned.1.call-done = f32[64,128,128]{2,1,0:T(8,128)} async-done(((f32[8,128,128]{2,1,0:T(8,128)}), f32[64,128,128]{2,1,0:T(8,128)}) %all-gather.7.cloned.1.call-update) | async-done | bytes 4194320 | tf_op jit(solution)/shard_map/all_gather | solution.py:22
  86.3 8.5 %while.30 = (s32[]{:T(128)}, f32[8,128,128]{2,1,0:T(8,128)S(1)}, s32[]{:T(128)}, f32[8,8]{1,0:T(8,128)S(1)}, f32[8,8,128,128]{3,2,1,0:T(8,128)}, /*index=5*/s32[]{:T(128)}, s32[]{:T(128)}) while((s32[]{:T(128)}, f32[8,128,128]{2,1,0:T(8,128)S(1)}, s32[]{:T(128)}, f32[8,8]{1,0:T(8,128)S(1)}, f32[8,8,128,128]{3,2,1,0:T(8,128)}, ...), condition=%wide.region_2.3_spmd.clone, body=%wide.region_1.2_spmd.clone.sunk | while | flops 524292 | bytes 1573073 | solution.py:31
  86.3 1.2 fusion.59
  87.5 1.2 fusion.59
  88.8 1.2 fusion.59
  90.0 1.2 fusion.59
  91.2 1.2 fusion.59
  92.4 1.2 fusion.59
  93.6 1.2 fusion.59
  95.4 4.8 %convolution_convert_fusion = bf16[128,3072]{1,0:T(8,128)(2,1)} fusion(bf16[128,1024]{0,1:T(8,128)(2,1)S(1)} %bitcast.135, bf16[1024,3072]{1,0:T(8,128)(2,1)} %param.14), kind=kOutput, calls=%fused_computation.6 | convolution fusion | flops 805699584 | bytes 7340032 | tf_op jit(solution)/shard_map/dot_general | solution.py:128
  100.3 36.4 %all-gather.9.cloned.1.call-done = bf16[64,128,128]{2,1,0:T(8,128)(2,1)} async-done(((bf16[8,128,128]{2,1,0:T(8,128)(2,1)}), bf16[64,128,128]{2,1,0:T(8,128)(2,1)}) %all-gather.9.cloned.1.call-update) | async-done | bytes 2097168 | tf_op jit(solution)/shard_map/all_gather | solution.py:37
  136.7 9.1 %while.31 = (s32[]{:T(128)}, f32[8,128,128]{2,1,0:T(8,128)S(1)}, s32[]{:T(128)}, bf16[8,8]{1,0:T(8,128)(2,1)S(1)}, bf16[8,8,128,128]{3,2,1,0:T(8,128)(2,1)}, /*index=5*/s32[]{:T(128)}, s32[]{:T(128)}, s32[]{:T(128)}, s32[]{:T(128)}) while((s32[]{:T(128)}, f32[8,128,128]{2,1,0:T(8,128)S(1)}, s32[]{:T(128)}, ...), condition=%wide.region_5.6_spmd.clone, body=%wide.region_4.5_spmd.clone.sunk | while | flops 655376 | bytes 1310975 | solution.py:55
  136.7 1.1 fusion.60
  137.8 1.1 fusion.60
  139.0 1.1 fusion.60
  140.1 1.1 fusion.60
  141.3 1.1 fusion.60
  142.4 1.1 fusion.60
  143.5 1.1 fusion.60
  144.7 1.1 fusion.60
  146.2 0.9 copy.122
  147.5 0.9 copy.123
  148.9 0.9 copy.121
  149.8 11.8 %reduce-scatter.2.cloned.1.call-done = bf16[128,768]{1,0:T(8,128)(2,1)} async-done(((bf16[128,3072]{1,0:T(8,128)(2,1)}), bf16[128,768]{1,0:T(8,128)(2,1)}) %reduce-scatter.2.cloned.1.call-update) | async-done | bytes 196624 | tf_op jit(solution)/shard_map/reduce_scatter | solution.py:129
  (60 shorter events, 5.2 us)
Async XLA Ops:
  7.2 1.2 copy-start
  7.2 3.4 %copy-start.5 = (bf16[128,768]{1,0:T(8,128)(2,1)S(1)}, bf16[128,768]{1,0:T(8,128)(2,1)}, u32[]{:S(2)}) copy-start(bf16[128,768]{1,0:T(8,128)(2,1)} %param.15) | copy-start | bytes 589828
  7.2 79.1 %all-gather.7.cloned.1.call-start = ((), (), s32[]{:S(2)}) async-start(), calls=%async_computation.3 | async-start | bytes 4718592 | tf_op jit(solution)/shard_map/all_gather | solution.py:22
  10.8 5.5 %copy-start.4 = (bf16[128,1024]{1,0:T(8,128)(2,1)S(1)}, bf16[128,1024]{1,0:T(8,128)(2,1)}, u32[]{:S(2)}) copy-start(bf16[128,1024]{1,0:T(8,128)(2,1)} %param.10) | copy-start | bytes 786436
  10.8 44.2 %copy-start.1 = (bf16[128,1024]{1,0:T(8,128)(2,1)S(1)}, bf16[128,1024]{1,0:T(8,128)(2,1)}, u32[]{:S(2)}) copy-start(bf16[128,1024]{1,0:T(8,128)(2,1)} %param.11) | copy-start | bytes 786436
  12.0 44.1 %all-to-all-start = ((bf16[128,4,768]{2,0,1:T(8,128)(2,1)}), bf16[128,4,768]{2,0,1:T(8,128)(2,1)S(1)}, u32[]{:S(2)}, u32[]{:S(2)}) async-start(bf16[128,4,768]{2,0,1:T(8,128)(2,1)} %copy.109), calls=%async_computation.1 | async-start | bytes 1572864 | tf_op jit(solution)/shard_map/all_to_all | solution.py:11
  16.3 120.4 %all-gather.9.cloned.1.call-start = ((), (), s32[]{:S(2)}) async-start(), calls=%async_computation.4 | async-start | bytes 2359296 | tf_op jit(solution)/shard_map/all_gather | solution.py:37
  61.5 1.8 %copy-start.3 = (bf16[8,128,128]{2,1,0:T(8,128)(2,1)S(1)}, bf16[8,128,128]{2,1,0:T(8,128)(2,1)}, u32[]{:S(2)}) copy-start(bf16[8,128,128]{2,1,0:T(8,128)(2,1)} %fusion.7) | copy-start | bytes 786436
  63.3 98.3 %reduce-scatter.2.cloned.1.call-start = ((), (), s32[]{:S(2)}) async-start(), calls=%async_computation.2 | async-start | bytes 983040 | tf_op jit(solution)/shard_map/reduce_scatter | solution.py:129
  145.8 1.2 copy-start.2
Sparse Core Ops, SparseCore 0:
  10.7 75.5 all-gather.6
  89.0 47.6 all-gather.8
  139.8 21.7 reduce-scatter.1
